TPU v7x, 256 devices: a whole 4x4x8 slice. The times are simulated.
256 devices in a mesh: stream: 2 (over z_hi), dp: 16 (over x, y), tensor: 8 (over z_lo, core).
Axes of the slice: x: 4, y: 4, z: 8 (z_hi: 2, z_lo: 4; z = z_hi * 4 + z_lo), core: 2. Of those that a mesh axis runs over, the one named last changes fastest.
Arguments:
- hidden: bfloat16 [2, 256, 8192], P('stream', 'tensor', 'dp'), may hold values from -3 to 3
- cached_rotated_keys: bfloat16 [2, 256, 8, 256, 128], P('stream', 'dp', 'tensor'), may hold values from -6 to 6
- cached_values: bfloat16 [2, 256, 8, 256, 128], P('stream', 'dp', 'tensor'), may hold values from -18 to 18
- cache_lengths: int32 [2, 256], P('stream', 'dp'), may hold values from 1 to 256, as said below
- recent_ids: int32 [256, 128], replicated, may hold values from 0 to 65535
- guidance: float32 [256], replicated, may hold values from 1 to 3
- w_query: bfloat16 [8192, 8192], P('dp', 'tensor'), may hold values from -0.0625 to 0.0625
- key_value_weight: bfloat16 [8192, 2, 1024], P('dp', None, 'tensor'), may hold values from -0.0625 to 0.0625
- w_output: bfloat16 [8192, 8192], P('tensor', 'dp'), may hold values from -0.0625 to 0.0625
- norm_gain: bfloat16 [8192], P('dp'), may hold values from 0.5 to 1.5
- w_head: bfloat16 [8192, 65536], P(None, ('dp', 'tensor')), may hold values from -0.16503906 to 0.16503906
Outputs:
- guided_logprobs: float32 [256, 65536], P('stream', ('dp', 'tensor'))
Inputs may be any that keep to these rules, and one draw needn't show every extreme that they name: `cache_lengths`: every prompt has 1 to 256 filled slots in each stream; some prompt has all 256; lengths differ widely from one group of 16 prompts to the next.
All inputs are finite; a program needn't handle non-finite values.
Results may differ from a plain program's by a relative error of at most 0.0025.
Values may be sent and summed in bfloat16 or wider, within the bound.
A program may use at most 64 MiB of HBM per device.

v0:
```python
import jax
import jax.numpy as jnp
from jax import lax
from jax.sharding import PartitionSpec as P

MODEL_WIDTH = 8192
HEAD_SIZE = 128
rope_theta = 500000.0
penalty_step = 1.5
norm_eps = 1e-05


def partner_2(value, axis, distance):
    mask = 2**distance
    pairs = [(source, source ^ mask) for source in range(lax.axis_size(axis))]
    return lax.ppermute(value, axis, pairs)


def rotate(values, positions):
    halfway = values.shape[-1] // 2
    frequency = rope_theta ** (-(jnp.arange(halfway, dtype=jnp.float32) * 2.0 / values.shape[-1]))
    angles = positions.astype(jnp.float32)[:, None, None] * frequency
    cosine_term = jnp.cos(angles)
    sine_term = jnp.sin(angles)
    first_half = values[..., :halfway]
    second_half = values[..., halfway:]
    return jnp.concatenate(
        [
            first_half * cosine_term - second_half * sine_term,
            second_half * cosine_term + first_half * sine_term,
        ],
        axis=-1,
    )


def repeat_counts(recent_ids, first_column, width):
    columns = first_column + jnp.arange(width, dtype=jnp.int32)
    return jnp.sum((recent_ids[:, :, None] == columns[None, None, :]).astype(jnp.float32), 1)


def body(
    hidden,
    cached_rotated_keys,
    cached_values,
    cache_lengths,
    recent_ids,
    guidance,
    w_query,
    key_value_weight,
    w_output,
    norm_gain,
    w_head,
):
    local_width = hidden.shape[2]
    query_cols = w_query.shape[1]
    kv_cols = key_value_weight.shape[2]
    local_prompts = cache_lengths.shape[1]
    lengths = cache_lengths[0]
    vocab_local = w_head.shape[1]
    all_rows = lax.all_gather(hidden[0], "tensor", axis=0, tiled=True)
    kv_flat = key_value_weight.reshape(local_width, 2 * kv_cols)
    projected = lax.psum_scatter(
        jnp.concatenate(
            [
                jnp.dot(all_rows, w_query, preferred_element_type=jnp.float32),
                jnp.dot(all_rows, kv_flat, preferred_element_type=jnp.float32),
            ],
            axis=1,
        ),
        "dp",
        scatter_dimension=0,
        tiled=True,
    )
    query_heads = query_cols // HEAD_SIZE
    kv_heads = kv_cols // HEAD_SIZE
    rotated_query = rotate(
        projected[:, :query_cols].reshape(local_prompts, query_heads, HEAD_SIZE), lengths
    ).astype(jnp.bfloat16)
    key_value_rows = projected[:, query_cols:].reshape(local_prompts, 2, kv_heads, HEAD_SIZE)
    fresh_key = rotate(key_value_rows[:, 0], lengths).astype(jnp.bfloat16)
    value_new = key_value_rows[:, 1].astype(jnp.bfloat16)
    grouped_queries = rotated_query.reshape(
        local_prompts, kv_heads, query_heads // kv_heads, HEAD_SIZE
    )
    attention_scale = HEAD_SIZE ** (-0.5)
    key_block = cached_rotated_keys[0]
    value_block = cached_values[0]
    scores = (
        jnp.einsum(
            "pkgd,pksd->pkgs", grouped_queries, key_block, preferred_element_type=jnp.float32
        )
        * attention_scale
    )
    self_score = (
        jnp.einsum("pkgd,pkd->pkg", grouped_queries, fresh_key, preferred_element_type=jnp.float32)
        * attention_scale
    )
    valid = jnp.arange(key_block.shape[2], dtype=jnp.int32)[None, :] < lengths[:, None]
    exps = jnp.where(valid[:, None, None, :], jnp.exp(scores), 0.0)
    own_exp = jnp.exp(self_score)
    denominator = jnp.sum(exps, -1) + own_exp
    weights = (exps / denominator[..., None]).astype(jnp.bfloat16)
    own_weight = (own_exp / denominator).astype(jnp.bfloat16)
    attended = jnp.einsum(
        "pkgs,pksd->pkgd", weights, value_block, preferred_element_type=jnp.float32
    )
    attended = (
        attended
        + own_weight.astype(jnp.float32)[..., None] * value_new.astype(jnp.float32)[:, :, None, :]
    )
    attended = attended.reshape(local_prompts, query_cols).astype(jnp.bfloat16)
    partial_out = jnp.dot(
        lax.all_gather(attended, "dp", axis=0, tiled=True),
        w_output,
        preferred_element_type=jnp.float32,
    )
    output_sum = lax.psum_scatter(partial_out, "tensor", scatter_dimension=0, tiled=True)
    residual = (hidden[0].astype(jnp.float32) + output_sum).astype(jnp.bfloat16)
    widened = residual.astype(jnp.float32)
    squares = lax.psum(jnp.sum(widened * widened, 1), "dp")
    inverse = lax.rsqrt(squares / MODEL_WIDTH + norm_eps)
    normed = (widened * inverse[:, None] * norm_gain.astype(jnp.float32)).astype(jnp.bfloat16)
    normed_all = lax.all_gather(normed, "tensor", axis=0, tiled=True)
    logits = jnp.dot(
        lax.all_gather(normed_all, "dp", axis=1, tiled=True),
        w_head,
        preferred_element_type=jnp.float32,
    )
    stream_side = lax.axis_index("stream")
    half_rows = logits.shape[0] // 2
    mine_start = stream_side * half_rows
    other_start = (1 - stream_side) * half_rows
    column_base = lax.axis_index(("dp", "tensor")) * vocab_local
    mine = lax.dynamic_slice_in_dim(logits, mine_start, half_rows, 0)
    sending = lax.dynamic_slice_in_dim(logits, other_start, half_rows, 0)
    partner = partner_2(sending, "stream", 0)
    conditional = jnp.where(stream_side == 0, mine, partner)
    unconditional = jnp.where(stream_side == 0, partner, mine)
    guide = lax.dynamic_slice_in_dim(guidance, mine_start, half_rows, 0)[:, None]
    recent_mine = lax.dynamic_slice_in_dim(recent_ids, mine_start, half_rows, 0)
    guided = unconditional + guide * (conditional - unconditional)
    guided = guided - penalty_step * repeat_counts(recent_mine, column_base, vocab_local)
    totals = lax.psum(jnp.sum(jnp.exp(guided), 1), ("dp", "tensor"))
    return guided - jnp.log(totals)[:, None]


def solution(mesh):
    return jax.shard_map(
        body,
        mesh=mesh,
        in_specs=(
            P("stream", "tensor", "dp"),
            P("stream", "dp", "tensor", None, None),
            P("stream", "dp", "tensor", None, None),
            P("stream", "dp"),
            P(),
            P(),
            P("dp", "tensor"),
            P("dp", None, "tensor"),
            P("tensor", "dp"),
            P("dp"),
            P(None, ("dp", "tensor")),
        ),
        out_specs=P("stream", ("dp", "tensor")),
        check_vma=False,
    )
```

profile of v0, /device:TPU:128, one launch (start us, length us, event | category | flops | bytes accessed | tf_op | source)
XLA Modules:
  0.0 647.4 jit_solution(1154850240006349418)
XLA Ops:
  6.6 14.5 %all-gather = bf16[1,256,512]{2,1,0:T(8,128)(2,1)S(1)} all-gather(bf16[1,32,512]{2,1,0:T(8,128)(2,1)} %param.11), channel_id=2, replica_groups=mesh['stream'=2,'dp'=16,'tensor'=8] {'tensor'}, dimensions={1}, use_global_device_ids=true | all-gather | bytes 294912 | tf_op jit(solution)/shard_map/all_gather | solution.py:60
  21.1 0.5 fusion.9
  21.6 1.2 fusion.5
  22.8 1.2 pad_maximum_fusion
  24.1 0.7 bitcast_convert_fusion
  24.7 0.7 iota_compare_fusion
  25.6 79.2 %reduce-scatter.3.cloned.1.call-done = f32[16,1280]{1,0:T(8,128)} async-done(((f32[256,1280]{1,0:T(8,128)}), f32[16,1280]{1,0:T(8,128)}) %reduce-scatter.3.cloned.1.call-update) | async-done | bytes 81936 | tf_op jit(solution)/shard_map/reduce_scatter | solution.py:62
  104.8 0.7 slice.36
  105.7 0.8 slice_bitcast_fusion
  106.9 1.7 fusion.33
  108.7 0.3 fusion.2
  109.0 23.3 %all_gather.13 = bf16[256,1024]{1,0:T(8,128)(2,1)S(1)} all-gather(bf16[16,1024]{1,0:T(8,128)(2,1)S(1)} %bitcast.51), channel_id=1, replica_groups=mesh['stream'=2,'dp'=16,'tensor'=8] {'dp'}, dimensions={0}, use_global_device_ids=true | all-gather | bytes 557056 | tf_op jit(solution)/shard_map/all_gather | solution.py:113
  132.3 1.2 fusion.34
  133.6 32.9 %reduce-scatter.5.cloned.1.call-done = f32[32,512]{1,0:T(8,128)} async-done(((f32[256,512]{1,0:T(8,128)}), f32[32,512]{1,0:T(8,128)}) %reduce-scatter.5.cloned.1.call-update) | async-done | bytes 65552 | tf_op jit(solution)/shard_map/reduce_scatter | solution.py:117
  166.5 1.0 fusion.11
  167.5 40.3 %psum.14 = f32[32]{0:T(128)S(1)} all-reduce(f32[32]{0:T(128)S(1)} %fusion.11), channel_id=1, replica_groups=mesh['stream'=2,'dp'=16,'tensor'=8] {'dp'}, use_global_device_ids=true, to_apply=%region_4.5 | all-reduce | flops 32 | bytes 256 | tf_op jit(solution)/shard_map/psum | solution.py:120
  207.8 0.9 fusion.13
  208.7 15.3 %all_gather.14 = bf16[256,512]{1,0:T(8,128)(2,1)} all-gather(bf16[32,512]{1,0:T(8,128)(2,1)S(1)} %fusion.13), channel_id=1, replica_groups=mesh['stream'=2,'dp'=16,'tensor'=8] {'tensor'}, dimensions={0}, use_global_device_ids=true | all-gather | bytes 294912 | tf_op jit(solution)/shard_map/all_gather | solution.py:123
  224.2 58.3 %all-gather.3.cloned.1.call-done = bf16[256,8192]{1,0:T(8,128)(2,1)} async-done(((bf16[256,512]{1,0:T(8,128)(2,1)}), bf16[256,8192]{1,0:T(8,128)(2,1)}) %all-gather.3.cloned.1.call-update) | async-done | bytes 4194320 | tf_op jit(solution)/shard_map/all_gather | solution.py:125
  282.5 7.0 %fusion.35 = f32[256,512]{1,0:T(8,128)S(1)} fusion(bf16[256,8192]{1,0:T(8,128)(2,1)} %all-gather.3.cloned.1.call-done, bf16[8192,512]{1,0:T(8,128)(2,1)} %param.21), kind=kOutput, calls=%fused_computation.66 | convolution fusion | flops 2147483648 | bytes 13107200 | tf_op jit(solution)/shard_map/dot_general | solution.py:124
  289.8 4.7 convert_reduce_fusion
  294.4 11.4 %collective-permute-done = f32[128,512]{1,0:T(8,128)S(1)} collective-permute-done((f32[128,512]{1,0:T(8,128)S(1)}, f32[128,512]{1,0:T(8,128)S(1)}, u32[]{:S(2)}, u32[]{:S(2)}) %collective-permute-start) | collective-permute-done | bytes 262176 | tf_op jit(solution)/shard_map/ppermute | solution.py:16
  306.0 334.1 %psum.15 = f32[128]{0:T(128)S(1)} all-reduce(f32[128]{0:T(128)S(1)} %get-tuple-element.5), channel_id=1, replica_groups=mesh['stream'=2,'dp'=16,'tensor'=8] {'dp','tensor'}, use_global_device_ids=true, to_apply=%region_7.8 | all-reduce | flops 128 | bytes 1024 | tf_op jit(solution)/shard_map/psum | solution.py:143
  640.1 0.8 broadcast_subtract_fusion
  (41 shorter events, 1.5 us)
Async XLA Ops:
  6.5 14.6 %copy-start = (bf16[512,1024]{1,0:T(8,128)(2,1)S(1)}, bf16[512,1024]{1,0:T(8,128)(2,1)}, u32[]{:S(2)}) copy-start(bf16[512,1024]{1,0:T(8,128)(2,1)} %param.17) | copy-start | bytes 3145732
  6.5 160.0 %copy-start.3 = (bf16[1,32,512]{2,1,0:T(8,128)(2,1)S(1)}, bf16[1,32,512]{2,1,0:T(8,128)(2,1)}, u32[]{:S(2)}) copy-start(bf16[1,32,512]{2,1,0:T(8,128)(2,1)} %param.11) | copy-start | bytes 98308
  6.5 102.2 %copy-start.1 = (bf16[1,16,1,256,128]{4,3,2,1,0:T(8,128)(2,1)S(1)}, bf16[1,16,1,256,128]{4,3,2,1,0:T(8,128)(2,1)}, u32[]{:S(2)}) copy-start(bf16[1,16,1,256,128]{4,3,2,1,0:T(8,128)(2,1)} %param.13) | copy-start | bytes 3145732
  6.5 125.8 %copy-start.2 = (bf16[1024,512]{1,0:T(8,128)(2,1)S(1)}, bf16[1024,512]{1,0:T(8,128)(2,1)}, u32[]{:S(2)}) copy-start(bf16[1024,512]{1,0:T(8,128)(2,1)} %param.19) | copy-start | bytes 3145732
  6.5 127.1 %copy-start.5 = (bf16[512]{0:T(512)(128)(2,1)S(1)}, bf16[512]{0:T(512)(128)(2,1)}, u32[]{:S(2)}) copy-start(bf16[512]{0:T(512)(128)(2,1)} %param.20) | copy-start | bytes 3076
  6.5 217.5 %copy-start.6 = (f32[256]{0:T(256)S(1)}, f32[256]{0:T(256)}, u32[]{:S(2)}) copy-start(f32[256]{0:T(256)} %param.16) | copy-start | bytes 3076
  6.6 217.6 %copy-start.4 = (s32[256,128]{1,0:T(8,128)S(1)}, s32[256,128]{1,0:T(8,128)}, u32[]{:S(2)}) copy-start(s32[256,128]{1,0:T(8,128)} %param.15) | copy-start | bytes 393220
  6.6 98.2 %reduce-scatter.3.cloned.1.call-start = ((), (), s32[]{:S(2)}) async-start(), calls=%async_computation.2 | async-start | bytes 1392640 | tf_op jit(solution)/shard_map/reduce_scatter | solution.py:62
  24.0 142.5 %reduce-scatter.5.cloned.1.call-start = ((), (), s32[]{:S(2)}) async-start(), calls=%async_computation.3 | async-start | bytes 589824 | tf_op jit(solution)/shard_map/reduce_scatter | solution.py:117
  133.6 148.9 %all-gather.3.cloned.1.call-start = ((), (), s32[]{:S(2)}) async-start(), calls=%async_computation.4 | async-start | bytes 4456448 | tf_op jit(solution)/shard_map/all_gather | solution.py:125
  289.5 16.3 %collective-permute-start = (f32[128,512]{1,0:T(8,128)S(1)}, f32[128,512]{1,0:T(8,128)S(1)}, u32[]{:S(2)}, u32[]{:S(2)}) collective-permute-start(f32[128,512]{1,0:T(8,128)S(1)} %constant_dynamic-slice_fusion.1), channel_id=1, source_target_pairs={{0,128},{128,0},{1,129},{129,1},{2,130},{130,2},{3,131},{131,3},{4... | collective-permute-start | bytes 786440 | tf_op jit(solution)/shard_map/ppermute | solution.py:16
Sparse Core Ops, SparseCore 0:
  24.1 80.6 reduce-scatter.2
  133.7 32.7 reduce-scatter.4
  224.2 58.2 all-gather.2
where the time goes:
time: 648 us; the launch traced here: 647 us
  blocking collectives  427 us (66%)
  waiting for transfers between devices  182 us (28%)
  between operations  13.3 us (2%)
  matrix products  12.1 us (2%)
  other arithmetic  10.5 us (2%)
    psum x1, blocking collectives, body(): totals = lax.psum(jnp.sum(jnp.exp(guided), 1), ('dp', 'tensor'))  334 us
    reduce_scatter x1, waiting for transfers between devices, body(): lax.psum_scatter(jnp.concatenate([jnp.dot(all_rows, w_query, preferred_el...  79.2 us
    all_gather x1, waiting for transfers between devices, body(): lax.all_gather(normed_all, 'dp', axis=1, tiled=True)  58.3 us
    psum x1, blocking collectives, body(): squares = lax.psum(jnp.sum(widened * widened, 1), 'dp')  40.3 us
    reduce_scatter x1, waiting for transfers between devices, body(): lax.psum_scatter(partial_out, 'tensor', scatter_dimension=0, tiled=True)  32.9 us
    all_gather x1, blocking collectives, body(): lax.all_gather(attended, 'dp', axis=0, tiled=True)  23.3 us
    all_gather x1, blocking collectives, body(): normed_all = lax.all_gather(normed, 'tensor', axis=0, tiled=True)  15.3 us
    all_gather x1, blocking collectives, body(): all_rows = lax.all_gather(hidden[0], 'tensor', axis=0, tiled=True)  14.5 us
  transfers between devices with their start and end apart: 4, of which 4 were waited for; matrix products, arithmetic and copies ran while one was open for 1% of the time, Pallas kernels for 0%

commit v1 on v0

--- a/solution.py
+++ b/solution.py
@@ -140,7 +140,8 @@
     recent_mine = lax.dynamic_slice_in_dim(recent_ids, mine_start, half_rows, 0)
     guided = unconditional + guide * (conditional - unconditional)
     guided = guided - penalty_step * repeat_counts(recent_mine, column_base, vocab_local)
-    totals = lax.psum(jnp.sum(jnp.exp(guided), 1), ("dp", "tensor"))
+    inner = lax.psum(jnp.sum(jnp.exp(guided), 1), "dp")
+    totals = lax.psum(inner, "tensor")
     return guided - jnp.log(totals)[:, None]
 
 

time: 648 us -> 367 us (0.57)
  blocking collectives: 427 us -> 145 us
    psum x1 -> x2, blocking collectives: 334 us -> 51.7 us  [the longest x1 38.1 us: body(): inner = lax.psum(jnp.sum(jnp.exp(guided), 1), 'dp')]
  transfers between devices with their start and end apart: 4 -> 4, of which waited for: 4 -> 4; matrix products, arithmetic and copies ran while one was open for 1% -> 2% of each run, Pallas kernels for 0% -> 0%
where the time goes in v1:
time: 367 us; the launch traced here: 365 us
  waiting for transfers between devices  182 us (50%)
  blocking collectives  145 us (40%)
  between operations  13.3 us (4%)
  matrix products  12.1 us (3%)
  other arithmetic  10.5 us (3%)
    reduce_scatter x1, waiting for transfers between devices, body(): lax.psum_scatter(jnp.concatenate([jnp.dot(all_rows, w_query, preferred_el...  79.2 us
    all_gather x1, waiting for transfers between devices, body(): lax.all_gather(normed_all, 'dp', axis=1, tiled=True)  58.3 us
    psum x1, blocking collectives, body(): squares = lax.psum(jnp.sum(widened * widened, 1), 'dp')  40.3 us
    psum x1, blocking collectives, body(): inner = lax.psum(jnp.sum(jnp.exp(guided), 1), 'dp')  38.1 us
    reduce_scatter x1, waiting for transfers between devices, body(): lax.psum_scatter(partial_out, 'tensor', scatter_dimension=0, tiled=True)  32.9 us
    all_gather x1, blocking collectives, body(): lax.all_gather(attended, 'dp', axis=0, tiled=True)  23.3 us
    all_gather x1, blocking collectives, body(): normed_all = lax.all_gather(normed, 'tensor', axis=0, tiled=True)  15.3 us
    all_gather x1, blocking collectives, body(): all_rows = lax.all_gather(hidden[0], 'tensor', axis=0, tiled=True)  14.5 us
  transfers between devices with their start and end apart: 4, of which 4 were waited for; matrix products, arithmetic and copies ran while one was open for 2% of the time, Pallas kernels for 0%

profile of v1, /device:TPU:128, one launch (start us, length us, event | category | flops | bytes accessed | tf_op | source)
XLA Modules:
  0.0 365.1 jit_solution(14583464911725139870)
XLA Ops:
  6.6 14.5 %all-gather = bf16[1,256,512]{2,1,0:T(8,128)(2,1)S(1)} all-gather(bf16[1,32,512]{2,1,0:T(8,128)(2,1)} %param.11), channel_id=2, replica_groups=mesh['stream'=2,'dp'=16,'tensor'=8] {'tensor'}, dimensions={1}, use_global_device_ids=true | all-gather | bytes 294912 | tf_op jit(solution)/shard_map/all_gather | solution.py:60
  21.1 0.5 fusion.9
  21.6 1.2 fusion.5
  22.8 1.2 pad_maximum_fusion
  24.1 0.7 bitcast_convert_fusion
  24.7 0.7 iota_compare_fusion
  25.6 79.2 %reduce-scatter.3.cloned.1.call-done = f32[16,1280]{1,0:T(8,128)} async-done(((f32[256,1280]{1,0:T(8,128)}), f32[16,1280]{1,0:T(8,128)}) %reduce-scatter.3.cloned.1.call-update) | async-done | bytes 81936 | tf_op jit(solution)/shard_map/reduce_scatter | solution.py:62
  104.8 0.7 slice.36
  105.7 0.8 slice_bitcast_fusion
  106.9 1.7 fusion.33
  109.0 23.3 %all_gather.13 = bf16[256,1024]{1,0:T(8,128)(2,1)S(1)} all-gather(bf16[16,1024]{1,0:T(8,128)(2,1)S(1)} %bitcast.51), channel_id=1, replica_groups=mesh['stream'=2,'dp'=16,'tensor'=8] {'dp'}, dimensions={0}, use_global_device_ids=true | all-gather | bytes 557056 | tf_op jit(solution)/shard_map/all_gather | solution.py:113
  132.3 1.2 fusion.34
  133.6 32.9 %reduce-scatter.5.cloned.1.call-done = f32[32,512]{1,0:T(8,128)} async-done(((f32[256,512]{1,0:T(8,128)}), f32[32,512]{1,0:T(8,128)}) %reduce-scatter.5.cloned.1.call-update) | async-done | bytes 65552 | tf_op jit(solution)/shard_map/reduce_scatter | solution.py:117
  166.5 1.0 fusion.11
  167.5 40.3 %psum.21 = f32[32]{0:T(128)S(1)} all-reduce(f32[32]{0:T(128)S(1)} %fusion.11), channel_id=1, replica_groups=mesh['stream'=2,'dp'=16,'tensor'=8] {'dp'}, use_global_device_ids=true, to_apply=%region_4.5 | all-reduce | flops 32 | bytes 256 | tf_op jit(solution)/shard_map/psum | solution.py:120
  207.8 0.9 fusion.13
  208.7 15.3 %all_gather.14 = bf16[256,512]{1,0:T(8,128)(2,1)} all-gather(bf16[32,512]{1,0:T(8,128)(2,1)S(1)} %fusion.13), channel_id=1, replica_groups=mesh['stream'=2,'dp'=16,'tensor'=8] {'tensor'}, dimensions={0}, use_global_device_ids=true | all-gather | bytes 294912 | tf_op jit(solution)/shard_map/all_gather | solution.py:123
  224.2 58.3 %all-gather.3.cloned.1.call-done = bf16[256,8192]{1,0:T(8,128)(2,1)} async-done(((bf16[256,512]{1,0:T(8,128)(2,1)}), bf16[256,8192]{1,0:T(8,128)(2,1)}) %all-gather.3.cloned.1.call-update) | async-done | bytes 4194320 | tf_op jit(solution)/shard_map/all_gather | solution.py:125
  282.5 7.0 %fusion.35 = f32[256,512]{1,0:T(8,128)S(1)} fusion(bf16[256,8192]{1,0:T(8,128)(2,1)} %all-gather.3.cloned.1.call-done, bf16[8192,512]{1,0:T(8,128)(2,1)} %param.21), kind=kOutput, calls=%fused_computation.66 | convolution fusion | flops 2147483648 | bytes 13107200 | tf_op jit(solution)/shard_map/dot_general | solution.py:124
  289.8 4.7 %convert_reduce_fusion = f32[128,512]{1,0:T(8,128)S(1)} fusion(s32[512]{0:T(512)S(1)} %iota_add_fusion, s32[128,128]{1,0:T(8,128)S(1)} %constant_dynamic-slice_fusion), kind=kLoop, calls=%fused_computation | loop fusion | flops 25100288 | bytes 329728 | tf_op jit(solution)/shard_map/reduce_sum | solution.py:38
  294.4 11.4 %collective-permute-done = f32[128,512]{1,0:T(8,128)S(1)} collective-permute-done((f32[128,512]{1,0:T(8,128)S(1)}, f32[128,512]{1,0:T(8,128)S(1)}, u32[]{:S(2)}, u32[]{:S(2)}) %collective-permute-start) | collective-permute-done | bytes 262176 | tf_op jit(solution)/shard_map/ppermute | solution.py:16
  306.0 38.1 %psum.22 = f32[128]{0:T(128)S(1)} all-reduce(f32[128]{0:T(128)S(1)} %get-tuple-element.5), channel_id=1, replica_groups=mesh['stream'=2,'dp'=16,'tensor'=8] {'dp'}, use_global_device_ids=true, to_apply=%region_7.8 | all-reduce | flops 128 | bytes 1024 | tf_op jit(solution)/shard_map/psum | solution.py:143
  344.1 13.6 %psum.23 = f32[128]{0:T(128)S(1)} all-reduce(f32[128]{0:T(128)S(1)} %psum.22), channel_id=1, replica_groups=mesh['stream'=2,'dp'=16,'tensor'=8] {'tensor'}, use_global_device_ids=true, to_apply=%region_8.9 | all-reduce | flops 128 | bytes 1024 | tf_op jit(solution)/shard_map/psum | solution.py:144
  357.7 0.8 broadcast_subtract_fusion
  (42 shorter events, 1.8 us)
Async XLA Ops:
  6.5 14.6 %copy-start = (bf16[512,1024]{1,0:T(8,128)(2,1)S(1)}, bf16[512,1024]{1,0:T(8,128)(2,1)}, u32[]{:S(2)}) copy-start(bf16[512,1024]{1,0:T(8,128)(2,1)} %param.17) | copy-start | bytes 3145732
  6.5 160.0 %copy-start.3 = (bf16[1,32,512]{2,1,0:T(8,128)(2,1)S(1)}, bf16[1,32,512]{2,1,0:T(8,128)(2,1)}, u32[]{:S(2)}) copy-start(bf16[1,32,512]{2,1,0:T(8,128)(2,1)} %param.11) | copy-start | bytes 98308
  6.5 102.2 %copy-start.1 = (bf16[1,16,1,256,128]{4,3,2,1,0:T(8,128)(2,1)S(1)}, bf16[1,16,1,256,128]{4,3,2,1,0:T(8,128)(2,1)}, u32[]{:S(2)}) copy-start(bf16[1,16,1,256,128]{4,3,2,1,0:T(8,128)(2,1)} %param.13) | copy-start | bytes 3145732
  6.5 125.8 %copy-start.2 = (bf16[1024,512]{1,0:T(8,128)(2,1)S(1)}, bf16[1024,512]{1,0:T(8,128)(2,1)}, u32[]{:S(2)}) copy-start(bf16[1024,512]{1,0:T(8,128)(2,1)} %param.19) | copy-start | bytes 3145732
  6.5 127.1 %copy-start.5 = (bf16[512]{0:T(512)(128)(2,1)S(1)}, bf16[512]{0:T(512)(128)(2,1)}, u32[]{:S(2)}) copy-start(bf16[512]{0:T(512)(128)(2,1)} %param.20) | copy-start | bytes 3076
  6.5 217.5 %copy-start.6 = (f32[256]{0:T(256)S(1)}, f32[256]{0:T(256)}, u32[]{:S(2)}) copy-start(f32[256]{0:T(256)} %param.16) | copy-start | bytes 3076
  6.6 217.6 %copy-start.4 = (s32[256,128]{1,0:T(8,128)S(1)}, s32[256,128]{1,0:T(8,128)}, u32[]{:S(2)}) copy-start(s32[256,128]{1,0:T(8,128)} %param.15) | copy-start | bytes 393220
  6.6 98.2 %reduce-scatter.3.cloned.1.call-start = ((), (), s32[]{:S(2)}) async-start(), calls=%async_computation.2 | async-start | bytes 1392640 | tf_op jit(solution)/shard_map/reduce_scatter | solution.py:62
  24.0 142.5 %reduce-scatter.5.cloned.1.call-start = ((), (), s32[]{:S(2)}) async-start(), calls=%async_computation.3 | async-start | bytes 589824 | tf_op jit(solution)/shard_map/reduce_scatter | solution.py:117
  133.6 148.9 %all-gather.3.cloned.1.call-start = ((), (), s32[]{:S(2)}) async-start(), calls=%async_computation.4 | async-start | bytes 4456448 | tf_op jit(solution)/shard_map/all_gather | solution.py:125
  289.5 16.3 %collective-permute-start = (f32[128,512]{1,0:T(8,128)S(1)}, f32[128,512]{1,0:T(8,128)S(1)}, u32[]{:S(2)}, u32[]{:S(2)}) collective-permute-start(f32[128,512]{1,0:T(8,128)S(1)} %constant_dynamic-slice_fusion.1), channel_id=1, source_target_pairs={{0,128},{128,0},{1,129},{129,1},{2,130},{130,2},{3,131},{131,3},{4... | collective-permute-start | bytes 786440 | tf_op jit(solution)/shard_map/ppermute | solution.py:16
Sparse Core Ops, SparseCore 0:
  24.1 80.6 reduce-scatter.2
  133.7 32.7 reduce-scatter.4
  224.2 58.2 all-gather.2
